TPU v7x, 32 devices: a whole 2x2x4 slice. The times are simulated.
32 devices in a mesh: tm: 2 (over x), grid: 16 (over z, y, core).
Axes of the slice: x: 2, y: 2, z: 4, core: 2. Of those that a mesh axis runs over, the one named last changes fastest.
Arguments:
- occupied_green: bfloat16 [2, 1024, 1024], P('tm', 'grid'), may hold values from -0.005859375 to 0.005859375
- empty_green: bfloat16 [2, 1024, 1024], P('tm', 'grid'), may hold values from -0.005859375 to 0.005859375
- basis: bfloat16 [12288, 1024], P('grid'), may hold values from -8 to 8
- time_weights: float32 [2, 2], replicated, may hold values from 0.25 to 1
Outputs:
- polarizability: float32 [2, 1024, 1024], P('tm', 'grid')
All inputs are finite; a program needn't handle non-finite values.
Results may differ from a plain program's by a relative error of at most 0.0012.
Values may be sent and summed in bfloat16 or wider, within the bound.
A program may use at most 128 MiB of HBM per device.

v0:
```python
import jax
import jax.numpy as jnp
from jax import lax
from jax.sharding import PartitionSpec as P

NR = 12288
NB = 1024


def weigh_times(time_weights, block_list, scale_factor):
    time_count = len(block_list)
    group_index = lax.axis_index("tm")
    weights_local = lax.dynamic_slice_in_dim(time_weights, group_index * time_count, time_count, 1)
    accum = weights_local[:, 0, None, None] * block_list[0][None]
    return scale_factor * accum


def step_size(piece_rows):
    return max((divisor for divisor in range(1, 2049) if piece_rows % divisor == 0))


def shards(occupied_green, empty_green, basis, time_weights):
    stacked = jnp.stack([occupied_green, empty_green])
    time_count = occupied_green.shape[0]
    coef_block = occupied_green.shape[1]
    row_total = basis.shape[0]
    scale_factor = 1.0 / NR

    def make_accumulate(combined_rows):

        def accumulate(running, basis_piece, first_row):
            piece_rows = basis_piece.shape[0]
            step_rows = step_size(piece_rows)

            def one_step(step_index, inner):
                basis_subpart = lax.dynamic_slice_in_dim(
                    basis_piece, step_index * step_rows, step_rows, 0
                )
                real_pair = jnp.einsum(
                    "qoa,ba->qob", combined_rows, basis_subpart, preferred_element_type=jnp.float32
                )
                product = (real_pair[0] * real_pair[1]).astype(jnp.bfloat16)
                return inner + jnp.dot(product, basis_subpart, preferred_element_type=jnp.float32)

            return lax.fori_loop(0, piece_rows // step_rows, one_step, running)

        return accumulate

    initial = jnp.zeros((time_count * row_total, NB), jnp.float32)
    projected = jnp.einsum(
        "sl,ftkl->ftsk",
        basis,
        lax.all_gather(stacked, "grid", axis=2, tiled=True),
        preferred_element_type=jnp.float32,
    ).astype(jnp.bfloat16)
    combined_rows = projected.reshape(2, time_count * row_total, NB)
    accumulate = make_accumulate(combined_rows)
    summed = accumulate(initial, lax.all_gather(basis, "grid", axis=0, tiled=True), jnp.int32(0))
    back_half = summed.astype(jnp.bfloat16).reshape(time_count, row_total, NB)
    coef_rows = lax.psum_scatter(
        jnp.einsum("tsk,sl->ktl", back_half, basis, preferred_element_type=jnp.float32).reshape(
            lax.axis_size("grid") * coef_block, time_count * NB
        ),
        "grid",
        scatter_dimension=0,
        tiled=True,
    ).reshape(coef_block, time_count, NB)
    block_list = [coef_rows[:, 0]]
    result = lax.psum_scatter(
        weigh_times(time_weights, block_list, scale_factor), "tm", scatter_dimension=0, tiled=True
    )
    return result


def solution(mesh):
    in_specs = (P("tm", "grid", None), P("tm", "grid", None), P("grid", None), P())
    out_specs = P("tm", "grid", None)
    return jax.shard_map(shards, mesh=mesh, in_specs=in_specs, out_specs=out_specs, check_vma=False)
```

profile of v0, /device:TPU:0, one launch (start us, length us, event | category | flops | bytes accessed | tf_op | source)
XLA Modules:
  0.0 431.6 jit_solution(16188916720244867342)
XLA Ops:
  6.5 0.0 copy-start
  6.5 0.0 all-gather.5.cloned.1.call-start
  6.5 1.7 pad_maximum_fusion
  8.2 0.0 all-gather.5.cloned.1.call-update
  8.3 0.0 all-gather.3.cloned.1.call-start
  8.3 0.7 all-gather.3.cloned.1.call-update
  9.0 0.0 reduce-scatter.3.cloned.1.call-start
  9.1 53.6 %all-gather.5.cloned.1.call-done = bf16[2,1,1024,1024]{3,2,0,1:T(8,128)(2,1)} async-done(((bf16[2,1,64,1024]{3,2,0,1:T(8,128)(2,1)}), bf16[2,1,1024,1024]{3,2,0,1:T(8,128)(2,1)}) %all-gather.5.cloned.1.call-update) | async-done | bytes 4194320 | tf_op jit(solution)/shard_map/all_gather | solution.py:53
  62.7 7.9 %convert_bitcast_fusion = bf16[2,768,1024]{1,2,0:T(8,128)(2,1)} fusion(bf16[2,1,1024,1024]{3,2,0,1:T(8,128)(2,1)} %all-gather.5.cloned.1.call-done, bf16[768,1024]{1,0:T(8,128)(2,1)} %param.8), kind=kOutput, calls=%fused_computation.13 | convolution fusion | flops 3222798336 | bytes 8912896 | tf_op jit(solution)/shard_map/sl,ftkl->ftsk/dot_general | solution.py:50
  70.5 3.2 copy.5
  73.8 117.6 %all-gather.3.cloned.1.call-done = bf16[12288,1024]{1,0:T(8,128)(2,1)} async-done(((bf16[768,1024]{1,0:T(8,128)(2,1)}), bf16[12288,1024]{1,0:T(8,128)(2,1)}) %all-gather.3.cloned.1.call-update) | async-done | bytes 25165840 | tf_op jit(solution)/shard_map/all_gather | solution.py:58
  191.3 138.8 %while.14 = (s32[]{:T(128)}, f32[768,1024]{1,0:T(8,128)}, bf16[12288,1024]{1,0:T(8,128)(2,1)}, bf16[2,768,1024]{2,1,0:T(8,128)(2,1)S(1)}, s32[]{:T(128)}, /*index=5*/s32[]{:T(128)}, s32[]{:T(128)}, s32[]{:T(128)}) while((s32[]{:T(128)}, f32[768,1024]{1,0:T(8,128)}, bf16[12288,1024]{1,0:T(8,128)(2,1)}, ...), condition=%wide.region_1.0_spmd.clone, body=%wide.region_0.0_spmd.clone.sunk | while | flops 9668395008 | bytes 42991772 | solution.py:45
  191.4 11.5 %convolution_bitcast_fusion.2 = f32[2,768,2048]{1,2,0:T(8,128)} fusion(bf16[2,768,1024]{2,1,0:T(8,128)(2,1)S(1)} %get-tuple-element.156, bf16[12288,1024]{1,0:T(8,128)(2,1)} %get-tuple-element.155, s32[]{:T(128)S(6)} %select_n.13), kind=kOutput, calls=%fused_computation.2.clone.1 | convolution fusion | flops 6442450944 | bytes 19922948 | tf_op jit(solution)/shard_map/while/body/eval_jaxpr/qoa,ba->qob/dot_general | solution.py:39
  202.9 10.9 %select_add_fusion.2 = f32[768,1024]{1,0:T(8,128)} fusion(f32[768,1024]{1,0:T(8,128)} %get-tuple-element.146, bf16[12288,1024]{1,0:T(8,128)(2,1)} %get-tuple-element.155, s32[]{:T(128)S(6)} %select_n.13, f32[2,768,2048]{1,2,0:T(8,128)} %convolution_bitcast_fusion.2, pred[]{:T(512)S(6)} %compare.3), kind=kOutput, calls=%fused_computation.8.clone.1 | convolution fusion | flops 3225944064 | bytes 23068676 | tf_op jit(solution)/shard_map/while/body/eval_jaxpr/dot_general | solution.py:43
  213.7 11.5 %convolution_bitcast_fusion.2 = f32[2,768,2048]{1,2,0:T(8,128)} fusion(bf16[2,768,1024]{2,1,0:T(8,128)(2,1)S(1)} %get-tuple-element.156, bf16[12288,1024]{1,0:T(8,128)(2,1)} %get-tuple-element.155, s32[]{:T(128)S(6)} %select_n.13), kind=kOutput, calls=%fused_computation.2.clone.1 | convolution fusion | flops 6442450944 | bytes 19922948 | tf_op jit(solution)/shard_map/while/body/eval_jaxpr/qoa,ba->qob/dot_general | solution.py:39
  225.2 11.8 %select_add_fusion.2 = f32[768,1024]{1,0:T(8,128)} fusion(f32[768,1024]{1,0:T(8,128)} %get-tuple-element.146, bf16[12288,1024]{1,0:T(8,128)(2,1)} %get-tuple-element.155, s32[]{:T(128)S(6)} %select_n.13, f32[2,768,2048]{1,2,0:T(8,128)} %convolution_bitcast_fusion.2, pred[]{:T(512)S(6)} %compare.3), kind=kOutput, calls=%fused_computation.8.clone.1 | convolution fusion | flops 3225944064 | bytes 23068676 | tf_op jit(solution)/shard_map/while/body/eval_jaxpr/dot_general | solution.py:43
  237.0 11.5 %convolution_bitcast_fusion.2 = f32[2,768,2048]{1,2,0:T(8,128)} fusion(bf16[2,768,1024]{2,1,0:T(8,128)(2,1)S(1)} %get-tuple-element.156, bf16[12288,1024]{1,0:T(8,128)(2,1)} %get-tuple-element.155, s32[]{:T(128)S(6)} %select_n.13), kind=kOutput, calls=%fused_computation.2.clone.1 | convolution fusion | flops 6442450944 | bytes 19922948 | tf_op jit(solution)/shard_map/while/body/eval_jaxpr/qoa,ba->qob/dot_general | solution.py:39
  248.5 11.8 %select_add_fusion.2 = f32[768,1024]{1,0:T(8,128)} fusion(f32[768,1024]{1,0:T(8,128)} %get-tuple-element.146, bf16[12288,1024]{1,0:T(8,128)(2,1)} %get-tuple-element.155, s32[]{:T(128)S(6)} %select_n.13, f32[2,768,2048]{1,2,0:T(8,128)} %convolution_bitcast_fusion.2, pred[]{:T(512)S(6)} %compare.3), kind=kOutput, calls=%fused_computation.8.clone.1 | convolution fusion | flops 3225944064 | bytes 23068676 | tf_op jit(solution)/shard_map/while/body/eval_jaxpr/dot_general | solution.py:43
  260.3 11.5 %convolution_bitcast_fusion.2 = f32[2,768,2048]{1,2,0:T(8,128)} fusion(bf16[2,768,1024]{2,1,0:T(8,128)(2,1)S(1)} %get-tuple-element.156, bf16[12288,1024]{1,0:T(8,128)(2,1)} %get-tuple-element.155, s32[]{:T(128)S(6)} %select_n.13), kind=kOutput, calls=%fused_computation.2.clone.1 | convolution fusion | flops 6442450944 | bytes 19922948 | tf_op jit(solution)/shard_map/while/body/eval_jaxpr/qoa,ba->qob/dot_general | solution.py:39
  271.8 11.8 %select_add_fusion.2 = f32[768,1024]{1,0:T(8,128)} fusion(f32[768,1024]{1,0:T(8,128)} %get-tuple-element.146, bf16[12288,1024]{1,0:T(8,128)(2,1)} %get-tuple-element.155, s32[]{:T(128)S(6)} %select_n.13, f32[2,768,2048]{1,2,0:T(8,128)} %convolution_bitcast_fusion.2, pred[]{:T(512)S(6)} %compare.3), kind=kOutput, calls=%fused_computation.8.clone.1 | convolution fusion | flops 3225944064 | bytes 23068676 | tf_op jit(solution)/shard_map/while/body/eval_jaxpr/dot_general | solution.py:43
  283.6 11.5 %convolution_bitcast_fusion.2 = f32[2,768,2048]{1,2,0:T(8,128)} fusion(bf16[2,768,1024]{2,1,0:T(8,128)(2,1)S(1)} %get-tuple-element.156, bf16[12288,1024]{1,0:T(8,128)(2,1)} %get-tuple-element.155, s32[]{:T(128)S(6)} %select_n.13), kind=kOutput, calls=%fused_computation.2.clone.1 | convolution fusion | flops 6442450944 | bytes 19922948 | tf_op jit(solution)/shard_map/while/body/eval_jaxpr/qoa,ba->qob/dot_general | solution.py:39
  295.1 11.8 %select_add_fusion.2 = f32[768,1024]{1,0:T(8,128)} fusion(f32[768,1024]{1,0:T(8,128)} %get-tuple-element.146, bf16[12288,1024]{1,0:T(8,128)(2,1)} %get-tuple-element.155, s32[]{:T(128)S(6)} %select_n.13, f32[2,768,2048]{1,2,0:T(8,128)} %convolution_bitcast_fusion.2, pred[]{:T(512)S(6)} %compare.3), kind=kOutput, calls=%fused_computation.8.clone.1 | convolution fusion | flops 3225944064 | bytes 23068676 | tf_op jit(solution)/shard_map/while/body/eval_jaxpr/dot_general | solution.py:43
  306.9 11.5 %convolution_bitcast_fusion.2 = f32[2,768,2048]{1,2,0:T(8,128)} fusion(bf16[2,768,1024]{2,1,0:T(8,128)(2,1)S(1)} %get-tuple-element.156, bf16[12288,1024]{1,0:T(8,128)(2,1)} %get-tuple-element.155, s32[]{:T(128)S(6)} %select_n.13), kind=kOutput, calls=%fused_computation.2.clone.1 | convolution fusion | flops 6442450944 | bytes 19922948 | tf_op jit(solution)/shard_map/while/body/eval_jaxpr/qoa,ba->qob/dot_general | solution.py:39
  318.4 11.8 %select_add_fusion.2 = f32[768,1024]{1,0:T(8,128)} fusion(f32[768,1024]{1,0:T(8,128)} %get-tuple-element.146, bf16[12288,1024]{1,0:T(8,128)(2,1)} %get-tuple-element.155, s32[]{:T(128)S(6)} %select_n.13, f32[2,768,2048]{1,2,0:T(8,128)} %convolution_bitcast_fusion.2, pred[]{:T(512)S(6)} %compare.3), kind=kOutput, calls=%fused_computation.8.clone.1 | convolution fusion | flops 3225944064 | bytes 23068676 | tf_op jit(solution)/shard_map/while/body/eval_jaxpr/dot_general | solution.py:43
  330.2 6.1 %fusion.18 = f32[1024,1024]{1,0:T(8,128)} fusion(bf16[768,1024]{1,0:T(8,128)(2,1)} %param.8, f32[768,1024]{1,0:T(8,128)} %get-tuple-element.84), kind=kOutput, calls=%fused_computation.15 | convolution fusion | flops 1611399168 | bytes 8912896 | tf_op jit(solution)/shard_map/tsk,sl->ktl/dot_general | solution.py:61
  336.3 0.0 reduce-scatter.3.cloned.1.call-update
  336.3 0.0 reduce-scatter.5.cloned.1.call-start
  336.4 0.0 copy-done
  336.4 0.2 dynamic-slice_reduce_fusion
  336.6 72.7 %reduce-scatter.3.cloned.1.call-done = f32[64,1024]{1,0:T(8,128)} async-done(((f32[1024,1024]{1,0:T(8,128)}), f32[64,1024]{1,0:T(8,128)}) %reduce-scatter.3.cloned.1.call-update) | async-done | bytes 262160 | tf_op jit(solution)/shard_map/reduce_scatter | solution.py:60
  409.2 1.9 multiply_multiply_fusion
  411.1 0.0 reduce-scatter.5.cloned.1.call-update
  411.1 13.9 %reduce-scatter.5.cloned.1.call-done = f32[1,64,1024]{2,1,0:T(8,128)} async-done(((f32[2,64,1024]{2,1,0:T(8,128)}), f32[1,64,1024]{2,1,0:T(8,128)}) %reduce-scatter.5.cloned.1.call-update) | async-done | bytes 262160 | tf_op jit(solution)/shard_map/reduce_scatter | solution.py:69
  (1 shorter events, 0.0 us)
Async XLA Ops:
  6.5 329.8 %copy-start = (f32[2,2]{1,0:T(2,128)S(1)}, f32[2,2]{1,0:T(2,128)}, u32[]{:S(2)}) copy-start(f32[2,2]{1,0:T(2,128)} %param.9) | copy-start | bytes 52
  6.5 56.1 %all-gather.5.cloned.1.call-start = ((), (), s32[]{:S(2)}) async-start(), calls=%async_computation.3 | async-start | bytes 4456448 | tf_op jit(solution)/shard_map/all_gather | solution.py:53
  8.3 183.1 %all-gather.3.cloned.1.call-start = ((), (), s32[]{:S(2)}) async-start(), calls=%async_computation.2 | async-start | bytes 26738688 | tf_op jit(solution)/shard_map/all_gather | solution.py:58
  9.0 400.2 %reduce-scatter.3.cloned.1.call-start = ((), (), s32[]{:S(2)}) async-start(), calls=%async_computation.4 | async-start | bytes 4456448 | tf_op jit(solution)/shard_map/reduce_scatter | solution.py:60
  336.3 88.8 %reduce-scatter.5.cloned.1.call-start = ((), (), s32[]{:S(2)}) async-start(), calls=%async_computation.5 | async-start | bytes 786432 | tf_op jit(solution)/shard_map/reduce_scatter | solution.py:69
Sparse Core Ops, SparseCore 0:
  9.5 53.1 all-gather.4
  64.3 127.0 all-gather.2
  336.4 72.7 reduce-scatter.2
  411.3 13.6 reduce-scatter.4
where the time goes:
time: 432 us
  waiting for transfers between devices  259 us (60%)
  matrix products  153 us (35%)
  between operations  13.2 us (3%)
    all_gather x1, waiting for transfers between devices, shards(): lax.all_gather(basis, 'grid', axis=0, tiled=True)  118 us
    reduce_scatter x1, waiting for transfers between devices, shards(): lax.psum_scatter(jnp.einsum('tsk,sl->ktl', back_half, basis, preferred_el...  72.7 us
    dot_general x6, matrix products, one_step(): jnp.dot(product, basis_subpart, preferred_element_type=jnp.float32)  69.8 us
    dot_general x6, matrix products, one_step(): jnp.einsum('qoa,ba->qob', combined_rows, basis_subpart, preferred_element...  69 us
    all_gather x1, waiting for transfers between devices, shards(): lax.all_gather(stacked, 'grid', axis=2, tiled=True)  53.6 us
    reduce_scatter x1, waiting for transfers between devices, shards(): lax.psum_scatter(weigh_times(time_weights, block_list, scale_factor), 'tm...  13.9 us
  transfers between devices with their start and end apart: 4, of which 4 were waited for; matrix products, arithmetic and copies ran while one was open for 3% of the time, Pallas kernels for 0%

commit v1 on v0

--- a/solution.py
+++ b/solution.py
@@ -50,7 +50,9 @@
     projected = jnp.einsum(
         "sl,ftkl->ftsk",
         basis,
-        lax.all_gather(stacked, "grid", axis=2, tiled=True),
+        jnp.concatenate(
+            lax.all_to_all(jnp.stack([stacked] * lax.axis_size("grid")), "grid", 0, 0), axis=2
+        ),
         preferred_element_type=jnp.float32,
     ).astype(jnp.bfloat16)
     combined_rows = projected.reshape(2, time_count * row_total, NB)

time: 432 us -> 470 us (1.088)
  waiting for transfers between devices: 259 us -> 288 us
  starting transfers between devices: 0.12 us -> 7.55 us
  local copies, waits for them, and re-layouts: 3.4 us -> 8.61 us
    all_to_all x0 -> x1, waiting for transfers between devices: none -> 141 us  [shards(): lax.all_to_all(jnp.stack([stacked] * lax.axis_size('grid')), 'grid', 0, 0)]
    all_gather x1, waiting for transfers between devices: 118 us -> 49.8 us  [shards(): lax.all_gather(basis, 'grid', axis=0, tiled=True)]
    all_gather x1 -> x0, waiting for transfers between devices: 53.6 us -> none  [shards(): lax.all_gather(stacked, 'grid', axis=2, tiled=True)]
    reduce_scatter x1, waiting for transfers between devices: 72.7 us -> 82 us  [shards(): lax.psum_scatter(jnp.einsum('tsk,sl->ktl', back_half, basis, preferred_el...]
    all_to_all x0 -> x1, starting transfers between devices: none -> 7.46 us  [shards(): lax.all_to_all(jnp.stack([stacked] * lax.axis_size('grid')), 'grid', 0, 0)]
where the time goes in v1:
time: 470 us
  waiting for transfers between devices  288 us (61%)
  matrix products  150 us (32%)
  between operations  13.2 us (3%)
  local copies, waits for them, and re-layouts  8.61 us (2%)
  starting transfers between devices  7.55 us (2%)
    all_to_all x1, waiting for transfers between devices, shards(): lax.all_to_all(jnp.stack([stacked] * lax.axis_size('grid')), 'grid', 0, 0)  141 us
    reduce_scatter x1, waiting for transfers between devices, shards(): lax.psum_scatter(jnp.einsum('tsk,sl->ktl', back_half, basis, preferred_el...  82 us
    dot_general x6, matrix products, one_step(): jnp.dot(product, basis_subpart, preferred_element_type=jnp.float32)  69.8 us
    dot_general x6, matrix products, one_step(): jnp.einsum('qoa,ba->qob', combined_rows, basis_subpart, preferred_element...  69 us
    all_gather x1, waiting for transfers between devices, shards(): lax.all_gather(basis, 'grid', axis=0, tiled=True)  49.8 us
    reduce_scatter x1, waiting for transfers between devices, shards(): lax.psum_scatter(weigh_times(time_weights, block_list, scale_factor), 'tm...  14.1 us
  transfers between devices with their start and end apart: 4, of which 4 were waited for; matrix products, arithmetic and copies ran while one was open for 3% of the time, Pallas kernels for 0%

profile of v1, /device:TPU:0, one launch (start us, length us, event | category | flops | bytes accessed | tf_op | source)
XLA Modules:
  0.0 469.6 jit_solution(2461877737687091937)
XLA Ops:
  6.5 0.0 copy-start
  6.5 0.0 all-gather.2.cloned.1.call-start
  6.5 0.7 all-gather.2.cloned.1.call-update
  7.3 1.0 maximum_bitcast_fusion
  8.3 2.5 stack.14
  10.7 7.5 %all-to-all-start = ((bf16[16,2,1,64,1024]{4,3,1,2,0:T(8,128)(2,1)}), bf16[16,2,1,64,1024]{4,3,1,2,0:T(8,128)(2,1)}, u32[]{:S(2)}, u32[]{:S(2)}) async-start(bf16[16,2,1,64,1024]{4,3,1,2,0:T(8,128)(2,1)} %stack.14), calls=%async_computation | async-start | bytes 8388608 | tf_op jit(solution)/shard_map/all_to_all | solution.py:54
  18.2 0.0 reduce-scatter.3.cloned.1.call-start
  18.3 141.0 %all-to-all-done = bf16[16,2,1,64,1024]{4,3,1,2,0:T(8,128)(2,1)} async-done(((bf16[16,2,1,64,1024]{4,3,1,2,0:T(8,128)(2,1)}), bf16[16,2,1,64,1024]{4,3,1,2,0:T(8,128)(2,1)}, u32[]{:S(2)}, u32[]{:S(2)}) %all-to-all-start) | async-done | bytes 4194336 | tf_op jit(solution)/shard_map/all_to_all | solution.py:54
  159.2 0.0 copy-start.1
  159.2 2.7 copy.6
  162.0 0.0 copy-done.1
  162.0 4.8 %convert_bitcast_fusion = bf16[2,768,1024]{1,2,0:T(8,128)(2,1)} fusion(bf16[2,1024,1024]{2,1,0:T(8,128)(2,1)S(1)} %bitcast.36, bf16[768,1024]{1,0:T(8,128)(2,1)S(1)} %copy-done.1), kind=kOutput, calls=%fused_computation.11 | convolution fusion | flops 3222798336 | bytes 8912896 | tf_op jit(solution)/shard_map/sl,ftkl->ftsk/dot_general | solution.py:50
  166.8 3.2 copy.7
  170.0 49.8 %all-gather.2.cloned.1.call-done = bf16[12288,1024]{1,0:T(8,128)(2,1)} async-done(((bf16[768,1024]{1,0:T(8,128)(2,1)}), bf16[12288,1024]{1,0:T(8,128)(2,1)}) %all-gather.2.cloned.1.call-update) | async-done | bytes 25165840 | tf_op jit(solution)/shard_map/all_gather | solution.py:60
  219.9 138.8 %while.14 = (s32[]{:T(128)}, f32[768,1024]{1,0:T(8,128)}, bf16[12288,1024]{1,0:T(8,128)(2,1)}, bf16[2,768,1024]{2,1,0:T(8,128)(2,1)S(1)}, s32[]{:T(128)}, /*index=5*/s32[]{:T(128)}, s32[]{:T(128)}, s32[]{:T(128)}) while((s32[]{:T(128)}, f32[768,1024]{1,0:T(8,128)}, bf16[12288,1024]{1,0:T(8,128)(2,1)}, ...), condition=%wide.region_1.0_spmd.clone, body=%wide.region_0.0_spmd.clone.sunk | while | flops 9668395008 | bytes 42991772 | solution.py:45
  219.9 11.5 %convolution_bitcast_fusion.2 = f32[2,768,2048]{1,2,0:T(8,128)} fusion(bf16[2,768,1024]{2,1,0:T(8,128)(2,1)S(1)} %get-tuple-element.160, bf16[12288,1024]{1,0:T(8,128)(2,1)} %get-tuple-element.159, s32[]{:T(128)S(6)} %select_n.13), kind=kOutput, calls=%fused_computation.2.clone.1 | convolution fusion | flops 6442450944 | bytes 19922948 | tf_op jit(solution)/shard_map/while/body/eval_jaxpr/qoa,ba->qob/dot_general | solution.py:39
  231.4 10.9 %select_add_fusion.2 = f32[768,1024]{1,0:T(8,128)} fusion(f32[768,1024]{1,0:T(8,128)} %get-tuple-element.150, bf16[12288,1024]{1,0:T(8,128)(2,1)} %get-tuple-element.159, s32[]{:T(128)S(6)} %select_n.13, f32[2,768,2048]{1,2,0:T(8,128)} %convolution_bitcast_fusion.2, pred[]{:T(512)S(6)} %compare.3), kind=kOutput, calls=%fused_computation.8.clone.1 | convolution fusion | flops 3225944064 | bytes 23068676 | tf_op jit(solution)/shard_map/while/body/eval_jaxpr/dot_general | solution.py:43
  242.3 11.5 %convolution_bitcast_fusion.2 = f32[2,768,2048]{1,2,0:T(8,128)} fusion(bf16[2,768,1024]{2,1,0:T(8,128)(2,1)S(1)} %get-tuple-element.160, bf16[12288,1024]{1,0:T(8,128)(2,1)} %get-tuple-element.159, s32[]{:T(128)S(6)} %select_n.13), kind=kOutput, calls=%fused_computation.2.clone.1 | convolution fusion | flops 6442450944 | bytes 19922948 | tf_op jit(solution)/shard_map/while/body/eval_jaxpr/qoa,ba->qob/dot_general | solution.py:39
  253.8 11.8 %select_add_fusion.2 = f32[768,1024]{1,0:T(8,128)} fusion(f32[768,1024]{1,0:T(8,128)} %get-tuple-element.150, bf16[12288,1024]{1,0:T(8,128)(2,1)} %get-tuple-element.159, s32[]{:T(128)S(6)} %select_n.13, f32[2,768,2048]{1,2,0:T(8,128)} %convolution_bitcast_fusion.2, pred[]{:T(512)S(6)} %compare.3), kind=kOutput, calls=%fused_computation.8.clone.1 | convolution fusion | flops 3225944064 | bytes 23068676 | tf_op jit(solution)/shard_map/while/body/eval_jaxpr/dot_general | solution.py:43
  265.5 11.5 %convolution_bitcast_fusion.2 = f32[2,768,2048]{1,2,0:T(8,128)} fusion(bf16[2,768,1024]{2,1,0:T(8,128)(2,1)S(1)} %get-tuple-element.160, bf16[12288,1024]{1,0:T(8,128)(2,1)} %get-tuple-element.159, s32[]{:T(128)S(6)} %select_n.13), kind=kOutput, calls=%fused_computation.2.clone.1 | convolution fusion | flops 6442450944 | bytes 19922948 | tf_op jit(solution)/shard_map/while/body/eval_jaxpr/qoa,ba->qob/dot_general | solution.py:39
  277.0 11.8 %select_add_fusion.2 = f32[768,1024]{1,0:T(8,128)} fusion(f32[768,1024]{1,0:T(8,128)} %get-tuple-element.150, bf16[12288,1024]{1,0:T(8,128)(2,1)} %get-tuple-element.159, s32[]{:T(128)S(6)} %select_n.13, f32[2,768,2048]{1,2,0:T(8,128)} %convolution_bitcast_fusion.2, pred[]{:T(512)S(6)} %compare.3), kind=kOutput, calls=%fused_computation.8.clone.1 | convolution fusion | flops 3225944064 | bytes 23068676 | tf_op jit(solution)/shard_map/while/body/eval_jaxpr/dot_general | solution.py:43
  288.8 11.5 %convolution_bitcast_fusion.2 = f32[2,768,2048]{1,2,0:T(8,128)} fusion(bf16[2,768,1024]{2,1,0:T(8,128)(2,1)S(1)} %get-tuple-element.160, bf16[12288,1024]{1,0:T(8,128)(2,1)} %get-tuple-element.159, s32[]{:T(128)S(6)} %select_n.13), kind=kOutput, calls=%fused_computation.2.clone.1 | convolution fusion | flops 6442450944 | bytes 19922948 | tf_op jit(solution)/shard_map/while/body/eval_jaxpr/qoa,ba->qob/dot_general | solution.py:39
  300.3 11.8 %select_add_fusion.2 = f32[768,1024]{1,0:T(8,128)} fusion(f32[768,1024]{1,0:T(8,128)} %get-tuple-element.150, bf16[12288,1024]{1,0:T(8,128)(2,1)} %get-tuple-element.159, s32[]{:T(128)S(6)} %select_n.13, f32[2,768,2048]{1,2,0:T(8,128)} %convolution_bitcast_fusion.2, pred[]{:T(512)S(6)} %compare.3), kind=kOutput, calls=%fused_computation.8.clone.1 | convolution fusion | flops 3225944064 | bytes 23068676 | tf_op jit(solution)/shard_map/while/body/eval_jaxpr/dot_general | solution.py:43
  312.1 11.5 %convolution_bitcast_fusion.2 = f32[2,768,2048]{1,2,0:T(8,128)} fusion(bf16[2,768,1024]{2,1,0:T(8,128)(2,1)S(1)} %get-tuple-element.160, bf16[12288,1024]{1,0:T(8,128)(2,1)} %get-tuple-element.159, s32[]{:T(128)S(6)} %select_n.13), kind=kOutput, calls=%fused_computation.2.clone.1 | convolution fusion | flops 6442450944 | bytes 19922948 | tf_op jit(solution)/shard_map/while/body/eval_jaxpr/qoa,ba->qob/dot_general | solution.py:39
  323.6 11.8 %select_add_fusion.2 = f32[768,1024]{1,0:T(8,128)} fusion(f32[768,1024]{1,0:T(8,128)} %get-tuple-element.150, bf16[12288,1024]{1,0:T(8,128)(2,1)} %get-tuple-element.159, s32[]{:T(128)S(6)} %select_n.13, f32[2,768,2048]{1,2,0:T(8,128)} %convolution_bitcast_fusion.2, pred[]{:T(512)S(6)} %compare.3), kind=kOutput, calls=%fused_computation.8.clone.1 | convolution fusion | flops 3225944064 | bytes 23068676 | tf_op jit(solution)/shard_map/while/body/eval_jaxpr/dot_general | solution.py:43
  335.4 11.5 %convolution_bitcast_fusion.2 = f32[2,768,2048]{1,2,0:T(8,128)} fusion(bf16[2,768,1024]{2,1,0:T(8,128)(2,1)S(1)} %get-tuple-element.160, bf16[12288,1024]{1,0:T(8,128)(2,1)} %get-tuple-element.159, s32[]{:T(128)S(6)} %select_n.13), kind=kOutput, calls=%fused_computation.2.clone.1 | convolution fusion | flops 6442450944 | bytes 19922948 | tf_op jit(solution)/shard_map/while/body/eval_jaxpr/qoa,ba->qob/dot_general | solution.py:39
  346.9 11.8 %select_add_fusion.2 = f32[768,1024]{1,0:T(8,128)} fusion(f32[768,1024]{1,0:T(8,128)} %get-tuple-element.150, bf16[12288,1024]{1,0:T(8,128)(2,1)} %get-tuple-element.159, s32[]{:T(128)S(6)} %select_n.13, f32[2,768,2048]{1,2,0:T(8,128)} %convolution_bitcast_fusion.2, pred[]{:T(512)S(6)} %compare.3), kind=kOutput, calls=%fused_computation.8.clone.1 | convolution fusion | flops 3225944064 | bytes 23068676 | tf_op jit(solution)/shard_map/while/body/eval_jaxpr/dot_general | solution.py:43
  358.7 6.1 %fusion.14 = f32[1024,1024]{1,0:T(8,128)} fusion(bf16[768,1024]{1,0:T(8,128)(2,1)} %param.8, f32[768,1024]{1,0:T(8,128)} %get-tuple-element.84), kind=kOutput, calls=%fused_computation.13 | convolution fusion | flops 1611399168 | bytes 8912896 | tf_op jit(solution)/shard_map/tsk,sl->ktl/dot_general | solution.py:63
  364.8 0.0 reduce-scatter.3.cloned.1.call-update
  364.8 0.0 reduce-scatter.5.cloned.1.call-start
  364.9 0.0 copy-done
  364.9 0.2 dynamic-slice_reduce_fusion
  365.1 82.0 %reduce-scatter.3.cloned.1.call-done = f32[64,1024]{1,0:T(8,128)} async-done(((f32[1024,1024]{1,0:T(8,128)}), f32[64,1024]{1,0:T(8,128)}) %reduce-scatter.3.cloned.1.call-update) | async-done | bytes 262160 | tf_op jit(solution)/shard_map/reduce_scatter | solution.py:62
  447.1 1.9 multiply_multiply_fusion
  448.9 0.0 reduce-scatter.5.cloned.1.call-update
  448.9 14.1 %reduce-scatter.5.cloned.1.call-done = f32[1,64,1024]{2,1,0:T(8,128)} async-done(((f32[2,64,1024]{2,1,0:T(8,128)}), f32[1,64,1024]{2,1,0:T(8,128)}) %reduce-scatter.5.cloned.1.call-update) | async-done | bytes 262160 | tf_op jit(solution)/shard_map/reduce_scatter | solution.py:71
  (1 shorter events, 0.0 us)
Async XLA Ops:
  6.5 358.4 %copy-start = (f32[2,2]{1,0:T(2,128)S(1)}, f32[2,2]{1,0:T(2,128)}, u32[]{:S(2)}) copy-start(f32[2,2]{1,0:T(2,128)} %param.9) | copy-start | bytes 52
  6.5 213.3 %all-gather.2.cloned.1.call-start = ((), (), s32[]{:S(2)}) async-start(), calls=%async_computation.3 | async-start | bytes 26738688 | tf_op jit(solution)/shard_map/all_gather | solution.py:60
  10.7 148.5 %all-to-all-start = ((bf16[16,2,1,64,1024]{4,3,1,2,0:T(8,128)(2,1)}), bf16[16,2,1,64,1024]{4,3,1,2,0:T(8,128)(2,1)}, u32[]{:S(2)}, u32[]{:S(2)}) async-start(bf16[16,2,1,64,1024]{4,3,1,2,0:T(8,128)(2,1)} %stack.14), calls=%async_computation | async-start | bytes 8388608 | tf_op jit(solution)/shard_map/all_to_all | solution.py:54
  18.2 428.9 %reduce-scatter.3.cloned.1.call-start = ((), (), s32[]{:S(2)}) async-start(), calls=%async_computation.4 | async-start | bytes 4456448 | tf_op jit(solution)/shard_map/reduce_scatter | solution.py:62
  159.2 2.8 copy-start.1
  364.8 98.2 %reduce-scatter.5.cloned.1.call-start = ((), (), s32[]{:S(2)}) async-start(), calls=%async_computation.5 | async-start | bytes 786432 | tf_op jit(solution)/shard_map/reduce_scatter | solution.py:71
Sparse Core Ops, SparseCore 0:
  8.9 210.8 all-gather.1
  364.9 82.0 reduce-scatter.2
  449.3 13.6 reduce-scatter.4
